TPU v7x, 32 devices: a whole 2x2x4 slice. The times are simulated.
32 devices in a mesh: dp: 8 (over z, x), tensor: 4 (over y, core).
Axes of the slice: x: 2, y: 2, z: 4, core: 2. Of those that a mesh axis runs over, the one named last changes fastest.
Arguments:
- tokens: bfloat16 [4096, 4096], P(('dp', 'tensor')), may hold values from -6 to 6
- norm_gain: float32 [4096], replicated, may hold values from 0.1 to 1.9
- w_query: bfloat16 [4096, 2048], P(None, 'tensor'), may hold values from -2 to 2
- key_weight: bfloat16 [4096, 512], P(None, 'tensor'), may hold values from -0.09375 to 0.09375
- value_weight: bfloat16 [4096, 512], P(None, 'tensor'), may hold values from -0.09375 to 0.09375
- w_out: bfloat16 [2048, 4096], P('tensor'), may hold values from -0.125 to 0.125
- lengths: int32 [4], replicated, may hold values from 1 to 2560, 4096 in all
Outputs:
- layer_out: bfloat16 [4096, 4096], P(('dp', 'tensor'))
Inputs may be any that keep to these rules, and one draw needn't show every extreme that they name: The lengths sum to 4096, and some document has exactly 2560 tokens.
All inputs are finite; a program needn't handle non-finite values.
Results may differ from a plain program's by a relative error of at most 0.0095.
The roundings to bfloat16 on the way count: a program that leaves them out, or rounds other values in their place, can miss the bound.
Values may be sent and summed in bfloat16 or wider, within the bound.
A program may use at most 128 MiB of HBM per device.

v0:
```python
import jax
import jax.numpy as jnp
from jax import lax
from jax.sharding import PartitionSpec as P

HEAD_SIZE = 128
epsilon = 1e-05
rope_base = 500000.0
masked = -1e30
initial_peak = -1e29


def from_behind(block, axis, distance):
    devices = range(lax.axis_size(axis))
    route = [(i - distance, i) for i in devices if i - distance in devices]
    return lax.ppermute(block, axis, route)


def doc_starts(lengths, positions):
    doc_ends = jnp.cumsum(lengths)
    closed = (doc_ends[None, :] <= positions[:, None]).astype(jnp.int32)
    return jnp.sum(closed * lengths[None, :], axis=1)


def rotate(vectors, offsets):
    half_width = vectors.shape[-1] // 2
    exponent = jnp.arange(half_width, dtype=jnp.float32) * (-2.0 / vectors.shape[-1])
    frequency = rope_base**exponent
    angles = offsets.astype(jnp.float32)[:, None] * frequency[None, :]
    cos_part = jnp.cos(angles)[:, None, :]
    sin_part = jnp.sin(angles)[:, None, :]
    leading = vectors[..., :half_width]
    trailing = vectors[..., half_width:]
    return jnp.concatenate(
        [leading * cos_part - trailing * sin_part, trailing * cos_part + leading * sin_part],
        axis=-1,
    )


def project(tokens, norm_gain, w_query, key_weight, value_weight, positions, starts):
    count = tokens.shape[0]
    wide = tokens.astype(jnp.float32)
    inverse = lax.rsqrt(jnp.mean(wide * wide, axis=1, keepdims=True) + epsilon)
    normed = (wide * inverse * norm_gain[None, :]).astype(jnp.bfloat16)
    offsets = positions - starts
    query_rows = jnp.dot(normed, w_query, preferred_element_type=jnp.float32).reshape(
        count, -1, HEAD_SIZE
    )
    query_rows = rotate(query_rows, offsets).astype(jnp.bfloat16)
    key = jnp.dot(normed, key_weight, preferred_element_type=jnp.float32).reshape(
        count, -1, HEAD_SIZE
    )
    key = rotate(key, offsets).astype(jnp.bfloat16)
    value_rows = jnp.dot(normed, value_weight, preferred_element_type=jnp.float32).astype(
        jnp.bfloat16
    )
    return (query_rows, key.reshape(count, -1), value_rows)


def attend_block(carry, keys, values, first_key, context):
    query_rows, positions, starts = context
    length = keys.shape[0]
    heads = query_rows.shape[1]
    key_pos = first_key + jnp.arange(length, dtype=jnp.int32)
    useful = (first_key + length - 1 >= starts[0]) & (first_key <= positions[-1])
    scale = query_rows.shape[-1] ** (-0.5)

    def compute(state):
        peak, mass, summed = state
        key_view = keys.reshape(length, heads, -1)
        value_view = values.reshape(length, heads, -1)
        scores = (
            jnp.einsum("qkgd,skd->qkgs", query_rows, key_view, preferred_element_type=jnp.float32)
            * scale
        )
        visible = (key_pos[None, :] >= starts[:, None]) & (key_pos[None, :] <= positions[:, None])
        scores = jnp.where(visible[:, None, None, :], scores, masked)
        fresh = jnp.maximum(peak, jnp.max(scores, axis=-1))
        shrink = jnp.exp(peak - fresh)
        probs = jnp.exp(scores - fresh[..., None])
        mass = mass * shrink + jnp.sum(probs, axis=-1)
        update = jnp.einsum(
            "qkgs,skd->qkgd",
            probs.astype(jnp.bfloat16),
            value_view,
            preferred_element_type=jnp.float32,
        )
        summed = summed * shrink[..., None] + update
        return (fresh, mass, summed)

    def unchanged(state):
        return state

    return lax.cond(useful, compute, unchanged, carry)


def fold_keys(carry, pieces, start, context):
    keys, values = pieces
    width = keys.shape[0]
    size = min(width, 1024)
    whole = width // size

    def one_block(index, state):
        offset = (index * size).astype(jnp.int32)
        return attend_block(state, keys, values, start + offset, context)

    carry = lax.fori_loop(0, whole, one_block, carry)
    return carry


def body(tokens, norm_gain, w_query, key_weight, value_weight, w_out, lengths):
    gathered = lax.all_gather(tokens, "tensor", axis=0, tiled=True)
    count = gathered.shape[0]
    first = lax.axis_index("dp") * count
    positions = first + jnp.arange(count, dtype=jnp.int32)
    starts = doc_starts(lengths, positions)
    query_rows, key, value_rows = project(
        gathered, norm_gain, w_query, key_weight, value_weight, positions, starts
    )
    heads = key.shape[1] // HEAD_SIZE
    query_rows = query_rows.reshape(count, heads, -1, HEAD_SIZE)
    group_count = query_rows.shape[2]
    context = (query_rows, positions, starts)
    initial = (
        jnp.full((count, heads, group_count), initial_peak, jnp.float32),
        jnp.zeros((count, heads, group_count), jnp.float32),
        jnp.zeros((count, heads, group_count, HEAD_SIZE), jnp.float32),
    )
    carry = fold_keys(initial, (key, value_rows), first, context)
    paired = jnp.stack([key, value_rows])
    reach = lax.axis_size("dp") // 2 + 1

    def one_step(back, state):
        moving, accum = state
        moving = from_behind(moving, "dp", 1)
        accum = fold_keys(accum, (moving[0], moving[1]), first - back * count, context)
        return (moving, accum)

    paired, carry = lax.fori_loop(1, reach + 1, one_step, (paired, carry))
    peak, mass, summed = carry
    attended = (summed / mass[..., None]).reshape(count, -1).astype(jnp.bfloat16)
    branch = lax.psum_scatter(
        jnp.dot(attended, w_out, preferred_element_type=jnp.float32).astype(jnp.bfloat16),
        "tensor",
        scatter_dimension=0,
        tiled=True,
    ).astype(jnp.float32)
    return (tokens.astype(jnp.float32) + branch).astype(jnp.bfloat16)


def solution(mesh):
    in_specs = (
        P(("dp", "tensor"), None),
        P(),
        P(None, "tensor"),
        P(None, "tensor"),
        P(None, "tensor"),
        P("tensor", None),
        P(),
    )
    out_specs = P(("dp", "tensor"), None)
    return jax.shard_map(body, mesh=mesh, in_specs=in_specs, out_specs=out_specs, check_vma=False)
```

profile of v0, /device:TPU:0, one launch (start us, length us, event | category | flops | bytes accessed | tf_op | source)
XLA Modules:
  0.0 201.6 jit_solution(4432884227593100175)
XLA Ops:
  6.5 0.0 copy-start
  6.5 0.0 all-gather.2.cloned.1.call-start
  6.5 0.7 all-gather.2.cloned.1.call-update
  7.3 0.0 reduce-scatter.2.cloned.1.call-start
  7.3 0.0 copy-start.8
  7.3 0.7 slice.69
  8.0 0.8 reduce-window.8
  8.8 0.7 select_reduce_fusion
  9.6 0.5 slice.68
  11.5 1.0 broadcast_in_dim.24
  12.5 0.0 copy-done.9
  12.5 1.8 multiply_cosine_fusion
  14.3 31.8 %all-gather.2.cloned.1.call-done = bf16[512,4096]{1,0:T(8,128)(2,1)} async-done(((bf16[128,4096]{1,0:T(8,128)(2,1)}), bf16[512,4096]{1,0:T(8,128)(2,1)}) %all-gather.2.cloned.1.call-update) | async-done | bytes 4194320 | tf_op jit(solution)/shard_map/all_gather | solution.py:112
  46.1 3.2 %fusion.42 = f32[512]{0:T(512)S(1)} fusion(bf16[512,4096]{1,0:T(8,128)(2,1)} %all-gather.2.cloned.1.call-done), kind=kLoop, calls=%fused_computation.47 | loop fusion | flops 6290944 | bytes 4196352 | tf_op jit(solution)/shard_map/reduce_sum | solution.py:43
  49.4 0.0 copy-done
  49.4 0.2 copy-done.2
  49.6 1.6 convolution_bitcast_fusion
  51.2 0.6 fusion.52
  51.8 1.6 convolution_convert_fusion.1
  53.4 0.0 copy-start.10
  53.5 0.8 copy.32
  54.3 5.9 %fusion.55 = f32[512,512]{0,1:T(8,128)S(1)} fusion(bf16[4096,512]{1,0:T(8,128)(2,1)} %param.15, bf16[512,4096]{1,0:T(8,128)(2,1)} %all-gather.2.cloned.1.call-done, f32[4096]{0:T(1024)S(1)} %copy-done.13, f32[512]{0:T(512)S(1)} %add_rsqrt_fusion), kind=kOutput, calls=%fused_computation.79 | convolution fusion | flops 2155872256 | bytes 9455616 | tf_op jit(solution)/shard_map/dot_general | solution.py:46
  60.2 0.9 fusion.59
  61.1 0.3 copy.40
  61.5 1.4 copy.39
  62.9 1.2 fusion.45
  64.1 0.3 pad_maximum_fusion
  64.4 5.8 %conditional.2 = ((f32[512,1,4]{0,2,1:T(4,128)S(1)}, f32[512,1,4]{0,2,1:T(4,128)S(1)}, f32[512,1,4,128]{3,0,2,1:T(8,128)})) conditional(s32[]{:T(128)} %convert_element_type.89, (f32[512,1,4]{0,2,1:T(4,128)S(1)}, f32[512,1,4]{0,2,1:T(4,128)S(1)}, f32[512,1,4,128]{3,0,2,1:T(8,128)}) %tuple.55, (s32[512]{0:T(512)}, s32[512]{0:T(512)}, ...), branch_computations={%region_3.4_spmd, %region_4.7_spmd} | conditional | flops 549722112 | bytes 25563252 | solution.py:94
  64.6 1.0 compare_and_fusion
  65.6 0.0 copy-start.3
  65.7 0.9 fusion.2
  66.6 0.9 fusion.1
  67.6 0.0 copy-done.3
  67.6 0.0 copy-done.11
  67.6 1.6 fusion.10
  69.2 0.0 copy-start.4
  69.2 1.0 copy-done.4
  70.2 56.5 %while.45 = (s32[]{:T(128)}, bf16[2,512,128]{2,1,0:T(8,128)(2,1)S(1)}, f32[512,1,4]{0,2,1:T(4,128)S(1)}, f32[512,1,4]{0,2,1:T(4,128)S(1)}, f32[512,1,4,128]{3,0,...) while((s32[]{:T(128)}, ...), condition=%wide.region_12.13_spmd, body=%wide.region_7.12_spmd.sunk | while | flops 549722624 | bytes 26620328 | solution.py:139
  70.2 3.4 %collective-permute-start = (bf16[2,512,128]{2,1,0:T(8,128)(2,1)S(1)}, bf16[2,512,128]{2,1,0:T(8,128)(2,1)S(1)}, u32[]{:S(2)}, u32[]{:S(2)}) collective-permute-start(bf16[2,512,128]{2,1,0:T(8,128)(2,1)S(1)} %get-tuple-element.655), channel_id=1, source_target_pairs={{0,4},{4,8},{8,12},{12,16},{16,20},{20,24},{24,28},{1,5},{5,9},{9,... | collective-permute-start | bytes 786440 | tf_op jit(solution)/shard_map/while/body/eval_jaxpr/ppermute | solution.py:16
  73.6 1.2 slice.94
  74.8 1.3 slice.95
  77.2 2.3 %collective-permute-done = bf16[2,512,128]{2,1,0:T(8,128)(2,1)S(1)} collective-permute-done((bf16[2,512,128]{2,1,0:T(8,128)(2,1)S(1)}, bf16[2,512,128]{2,1,0:T(8,128)(2,1)S(1)}, u32[]{:S(2)}, u32[]{:S(2)}) %collective-permute-start) | collective-permute-done | bytes 262176 | tf_op jit(solution)/shard_map/while/body/eval_jaxpr/ppermute | solution.py:16
  79.6 9.7 %collective-permute-start = (bf16[2,512,128]{2,1,0:T(8,128)(2,1)S(1)}, bf16[2,512,128]{2,1,0:T(8,128)(2,1)S(1)}, u32[]{:S(2)}, u32[]{:S(2)}) collective-permute-start(bf16[2,512,128]{2,1,0:T(8,128)(2,1)S(1)} %get-tuple-element.655), channel_id=1, source_target_pairs={{0,4},{4,8},{8,12},{12,16},{16,20},{20,24},{24,28},{1,5},{5,9},{9,... | collective-permute-start | bytes 786440 | tf_op jit(solution)/shard_map/while/body/eval_jaxpr/ppermute | solution.py:16
  89.3 1.2 slice.94
  90.5 1.3 slice.95
  92.9 1.4 collective-permute-done
  94.4 4.4 %collective-permute-start = (bf16[2,512,128]{2,1,0:T(8,128)(2,1)S(1)}, bf16[2,512,128]{2,1,0:T(8,128)(2,1)S(1)}, u32[]{:S(2)}, u32[]{:S(2)}) collective-permute-start(bf16[2,512,128]{2,1,0:T(8,128)(2,1)S(1)} %get-tuple-element.655), channel_id=1, source_target_pairs={{0,4},{4,8},{8,12},{12,16},{16,20},{20,24},{24,28},{1,5},{5,9},{9,... | collective-permute-start | bytes 786440 | tf_op jit(solution)/shard_map/while/body/eval_jaxpr/ppermute | solution.py:16
  98.8 1.2 slice.94
  100.0 1.3 slice.95
  102.5 0.6 collective-permute-done
  103.1 10.5 %collective-permute-start = (bf16[2,512,128]{2,1,0:T(8,128)(2,1)S(1)}, bf16[2,512,128]{2,1,0:T(8,128)(2,1)S(1)}, u32[]{:S(2)}, u32[]{:S(2)}) collective-permute-start(bf16[2,512,128]{2,1,0:T(8,128)(2,1)S(1)} %get-tuple-element.655), channel_id=1, source_target_pairs={{0,4},{4,8},{8,12},{12,16},{16,20},{20,24},{24,28},{1,5},{5,9},{9,... | collective-permute-start | bytes 786440 | tf_op jit(solution)/shard_map/while/body/eval_jaxpr/ppermute | solution.py:16
  113.6 1.2 slice.94
  114.8 1.3 slice.95
  117.3 0.2 collective-permute-done
  117.5 5.3 %collective-permute-start = (bf16[2,512,128]{2,1,0:T(8,128)(2,1)S(1)}, bf16[2,512,128]{2,1,0:T(8,128)(2,1)S(1)}, u32[]{:S(2)}, u32[]{:S(2)}) collective-permute-start(bf16[2,512,128]{2,1,0:T(8,128)(2,1)S(1)} %get-tuple-element.655), channel_id=1, source_target_pairs={{0,4},{4,8},{8,12},{12,16},{16,20},{20,24},{24,28},{1,5},{5,9},{9,... | collective-permute-start | bytes 786440 | tf_op jit(solution)/shard_map/while/body/eval_jaxpr/ppermute | solution.py:16
  122.8 1.2 slice.94
  124.0 1.3 slice.95
  126.5 0.2 collective-permute-done
  126.7 1.6 copy.33
  128.3 0.1 divide_convert_fusion
  128.4 6.5 %convolution_convert_fusion = bf16[512,4096]{1,0:T(8,128)(2,1)} fusion(bf16[512,512]{0,1:T(8,128)(2,1)S(1)} %bitcast.139, bf16[512,4096]{1,0:T(8,128)(2,1)} %param.18), kind=kOutput, calls=%fused_computation.50 | convolution fusion | flops 2149580800 | bytes 8912896 | tf_op jit(solution)/shard_map/dot_general | solution.py:143
  134.9 0.0 reduce-scatter.2.cloned.1.call-update
  134.9 57.3 %reduce-scatter.2.cloned.1.call-done = bf16[128,4096]{1,0:T(8,128)(2,1)} async-done(((bf16[512,4096]{1,0:T(8,128)(2,1)}), bf16[128,4096]{1,0:T(8,128)(2,1)}) %reduce-scatter.2.cloned.1.call-update) | async-done | bytes 1048592 | tf_op jit(solution)/shard_map/reduce_scatter | solution.py:142
  192.3 2.4 %add_convert_fusion = bf16[128,4096]{1,0:T(8,128)(2,1)} fusion(bf16[128,4096]{1,0:T(8,128)(2,1)} %reduce-scatter.2.cloned.1.call-done, bf16[128,4096]{1,0:T(8,128)(2,1)S(1)} %copy-done.1), kind=kLoop, calls=%fused_computation.51 | loop fusion | flops 2097152 | bytes 3145728 | tf_op jit(solution)/shard_map/convert_element_type | solution.py:148
  (39 shorter events, 0.2 us)
Async XLA Ops:
  6.5 42.8 %copy-start = (bf16[4096,128]{1,0:T(8,128)(2,1)S(1)}, bf16[4096,128]{1,0:T(8,128)(2,1)}, u32[]{:S(2)}) copy-start(bf16[4096,128]{1,0:T(8,128)(2,1)} %param.16) | copy-start | bytes 3145732
  6.5 42.8 %copy-start.13 = (f32[4096]{0:T(1024)S(1)}, f32[4096]{0:T(1024)}, u32[]{:S(2)}) copy-start(f32[4096]{0:T(1024)} %param.14) | copy-start | bytes 49156
  6.5 39.6 %all-gather.2.cloned.1.call-start = ((), (), s32[]{:S(2)}) async-start(), calls=%async_computation.1 | async-start | bytes 5242880 | tf_op jit(solution)/shard_map/all_gather | solution.py:112
  7.3 185.0 %reduce-scatter.2.cloned.1.call-start = ((), (), s32[]{:S(2)}) async-start(), calls=%async_computation.2 | async-start | bytes 5242880 | tf_op jit(solution)/shard_map/reduce_scatter | solution.py:142
  7.3 43.9 %copy-start.8 = (s32[512]{0:T(512)}, s32[512]{0:T(512)S(1)}, u32[]{:S(2)}) copy-start(s32[512]{0:T(512)S(1)} %iota_add_fusion) | copy-start | bytes 6148
  9.6 2.9 %copy-start.9 = (s32[512]{0:T(512)}, s32[512]{0:T(512)S(1)}, u32[]{:S(2)}) copy-start(s32[512]{0:T(512)S(1)} %select_reduce_fusion) | copy-start | bytes 6148
  46.1 3.4 %copy-start.2 = (bf16[512,4096]{1,0:T(8,128)(2,1)S(1)}, bf16[512,4096]{1,0:T(8,128)(2,1)}, u32[]{:S(2)}) copy-start(bf16[512,4096]{1,0:T(8,128)(2,1)} %all-gather.2.cloned.1.call-done) | copy-start | bytes 12582916
  49.6 2.2 %copy-start.12 = (bf16[4096,128]{1,0:T(8,128)(2,1)S(1)}, bf16[4096,128]{1,0:T(8,128)(2,1)}, u32[]{:S(2)}) copy-start(bf16[4096,128]{1,0:T(8,128)(2,1)} %param.17) | copy-start | bytes 3145732
  53.4 6.8 %copy-start.10 = (bf16[512,128]{0,1:T(8,128)(2,1)}, bf16[512,128]{0,1:T(8,128)(2,1)S(1)}, u32[]{:S(2)}) copy-start(bf16[512,128]{0,1:T(8,128)(2,1)S(1)} %convolution_convert_fusion.1) | copy-start | bytes 393220
  64.4 5.8 %copy-start.7 = (bf16[2,512,128]{2,1,0:T(8,128)(2,1)S(1)}, bf16[2,512,128]{2,1,0:T(8,128)(2,1)}, u32[]{:S(2)}) copy-start(bf16[2,512,128]{2,1,0:T(8,128)(2,1)} %copy.32) | copy-start | bytes 786436
  65.6 1.9 copy-start.3
  65.6 1.9 copy-start.11
  69.2 1.0 copy-start.4
  70.2 9.3 %collective-permute-start = (bf16[2,512,128]{2,1,0:T(8,128)(2,1)S(1)}, bf16[2,512,128]{2,1,0:T(8,128)(2,1)S(1)}, u32[]{:S(2)}, u32[]{:S(2)}) collective-permute-start(bf16[2,512,128]{2,1,0:T(8,128)(2,1)S(1)} %get-tuple-element.655), channel_id=1, source_target_pairs={{0,4},{4,8},{8,12},{12,16},{16,20},{20,24},{24,28},{1,5},{5,9},{9,... | collective-permute-start | bytes 786440 | tf_op jit(solution)/shard_map/while/body/eval_jaxpr/ppermute | solution.py:16
  79.6 14.8 %collective-permute-start = (bf16[2,512,128]{2,1,0:T(8,128)(2,1)S(1)}, bf16[2,512,128]{2,1,0:T(8,128)(2,1)S(1)}, u32[]{:S(2)}, u32[]{:S(2)}) collective-permute-start(bf16[2,512,128]{2,1,0:T(8,128)(2,1)S(1)} %get-tuple-element.655), channel_id=1, source_target_pairs={{0,4},{4,8},{8,12},{12,16},{16,20},{20,24},{24,28},{1,5},{5,9},{9,... | collective-permute-start | bytes 786440 | tf_op jit(solution)/shard_map/while/body/eval_jaxpr/ppermute | solution.py:16
  94.4 8.6 %collective-permute-start = (bf16[2,512,128]{2,1,0:T(8,128)(2,1)S(1)}, bf16[2,512,128]{2,1,0:T(8,128)(2,1)S(1)}, u32[]{:S(2)}, u32[]{:S(2)}) collective-permute-start(bf16[2,512,128]{2,1,0:T(8,128)(2,1)S(1)} %get-tuple-element.655), channel_id=1, source_target_pairs={{0,4},{4,8},{8,12},{12,16},{16,20},{20,24},{24,28},{1,5},{5,9},{9,... | collective-permute-start | bytes 786440 | tf_op jit(solution)/shard_map/while/body/eval_jaxpr/ppermute | solution.py:16
  103.1 14.4 %collective-permute-start = (bf16[2,512,128]{2,1,0:T(8,128)(2,1)S(1)}, bf16[2,512,128]{2,1,0:T(8,128)(2,1)S(1)}, u32[]{:S(2)}, u32[]{:S(2)}) collective-permute-start(bf16[2,512,128]{2,1,0:T(8,128)(2,1)S(1)} %get-tuple-element.655), channel_id=1, source_target_pairs={{0,4},{4,8},{8,12},{12,16},{16,20},{20,24},{24,28},{1,5},{5,9},{9,... | collective-permute-start | bytes 786440 | tf_op jit(solution)/shard_map/while/body/eval_jaxpr/ppermute | solution.py:16
  117.5 9.2 %collective-permute-start = (bf16[2,512,128]{2,1,0:T(8,128)(2,1)S(1)}, bf16[2,512,128]{2,1,0:T(8,128)(2,1)S(1)}, u32[]{:S(2)}, u32[]{:S(2)}) collective-permute-start(bf16[2,512,128]{2,1,0:T(8,128)(2,1)S(1)} %get-tuple-element.655), channel_id=1, source_target_pairs={{0,4},{4,8},{8,12},{12,16},{16,20},{20,24},{24,28},{1,5},{5,9},{9,... | collective-permute-start | bytes 786440 | tf_op jit(solution)/shard_map/while/body/eval_jaxpr/ppermute | solution.py:16
  134.9 57.4 %copy-start.1 = (bf16[128,4096]{1,0:T(8,128)(2,1)S(1)}, bf16[128,4096]{1,0:T(8,128)(2,1)}, u32[]{:S(2)}) copy-start(bf16[128,4096]{1,0:T(8,128)(2,1)} %param.13) | copy-start | bytes 3145732
Sparse Core Ops, SparseCore 0:
  8.9 37.1 all-gather.1
  135.1 57.1 reduce-scatter.1
where the time goes:
time: 202 us
  waiting for transfers between devices  94.5 us (47%)
  starting transfers between devices  33.3 us (16%)
  local copies, waits for them, and re-layouts  20.8 us (10%)
  matrix products  18.3 us (9%)
  between operations  14.9 us (7%)
  other arithmetic  13.2 us (7%)
  loops' own time  6.45 us (3%)
    reduce_scatter x1, waiting for transfers between devices, body(): lax.psum_scatter(jnp.dot(attended, w_out, preferred_element_type=jnp.floa...  57.3 us
    ppermute x5, starting transfers between devices, from_behind(): return lax.ppermute(block, axis, route)  33.3 us
    all_gather x1, waiting for transfers between devices, body(): gathered = lax.all_gather(tokens, 'tensor', axis=0, tiled=True)  31.8 us
    slice x6, local copies, waits for them, and re-layouts, attend_block(): positions[-1]  7.09 us
    dot_general x1, matrix products, body(): jnp.dot(attended, w_out, preferred_element_type=jnp.float32)  6.51 us
    slice x6, local copies, waits for them, and re-layouts, attend_block(): starts[0]  6.39 us
    another operation x1, loops' own time, body(): paired, carry = lax.fori_loop(1, reach + 1, one_step, (paired, carry))  6.17 us
    dot_general x1, matrix products, project(): jnp.dot(normed, w_query, preferred_element_type=jnp.float32)  5.94 us
  transfers between devices with their start and end apart: 7, of which 7 were waited for; matrix products, arithmetic and copies ran while one was open for 9% of the time, Pallas kernels for 0%

commit v1 on v0

--- a/solution.py
+++ b/solution.py
@@ -109,7 +109,8 @@
 
 
 def body(tokens, norm_gain, w_query, key_weight, value_weight, w_out, lengths):
-    gathered = lax.all_gather(tokens, "tensor", axis=0, tiled=True)
+    stack = jnp.stack([tokens] * lax.axis_size("tensor"))
+    gathered = jnp.concatenate(lax.all_to_all(stack, "tensor", 0, 0), axis=0)
     count = gathered.shape[0]
     first = lax.axis_index("dp") * count
     positions = first + jnp.arange(count, dtype=jnp.int32)

time: 202 us -> 215 us (1.064)
  waiting for transfers between devices: 94.5 us -> 105 us
  matrix products: 18.3 us -> 14.5 us
  other arithmetic: 13.2 us -> 16.3 us
  starting transfers between devices: 33.3 us -> 35.5 us
    all_to_all x0 -> x1, waiting for transfers between devices: none -> 39.3 us  [body(): gathered = jnp.concatenate(lax.all_to_all(stack, 'tensor', 0, 0), axis=0)]
    all_gather x1 -> x0, waiting for transfers between devices: 31.8 us -> none  [body(): gathered = lax.all_gather(tokens, 'tensor', axis=0, tiled=True)]
    convert_element_type x0 -> x2, other arithmetic: none -> 7.8 us  [project(): normed = (wide * inverse * norm_gain[None, :]).astype(jnp.bfloat16)]
    ppermute x5, waiting for transfers between devices: 4.62 us -> 11.3 us  [from_behind(): return lax.ppermute(block, axis, route)]
    dot_general x0 -> x1, local copies, waits for them, and re-layouts: none -> 6.39 us  [project(): jnp.dot(normed, w_query, preferred_element_type=jnp.float32)]
    all_to_all x0 -> x1, starting transfers between devices: none -> 4.97 us  [body(): gathered = jnp.concatenate(lax.all_to_all(stack, 'tensor', 0, 0), axis=0)]
    another operation x0 -> x1, local copies, waits for them, and re-layouts: none -> 3.79 us  [body(): stack = jnp.stack([tokens] * lax.axis_size('tensor'))]
    slice x6, local copies, waits for them, and re-layouts: 7.09 us -> 3.42 us  [attend_block(): positions[-1]]
  transfers between devices with their start and end apart: 7 -> 7, of which waited for: 7 -> 7; matrix products, arithmetic and copies ran while one was open for 9% -> 6% of each run, Pallas kernels for 0% -> 0%
where the time goes in v1:
time: 215 us; the launch traced here: 214 us
  waiting for transfers between devices  105 us (49%)
  starting transfers between devices  35.5 us (17%)
  local copies, waits for them, and re-layouts  21.8 us (10%)
  other arithmetic  16.3 us (8%)
  between operations  14.8 us (7%)
  matrix products  14.5 us (7%)
  loops' own time  6.27 us (3%)
    reduce_scatter x1, waiting for transfers between devices, body(): lax.psum_scatter(jnp.dot(attended, w_out, preferred_element_type=jnp.floa...  54.5 us
    all_to_all x1, waiting for transfers between devices, body(): gathered = jnp.concatenate(lax.all_to_all(stack, 'tensor', 0, 0), axis=0)  39.3 us
    ppermute x5, starting transfers between devices, from_behind(): return lax.ppermute(block, axis, route)  30.5 us
    ppermute x5, waiting for transfers between devices, from_behind(): return lax.ppermute(block, axis, route)  11.3 us
    convert_element_type x2, other arithmetic, project(): normed = (wide * inverse * norm_gain[None, :]).astype(jnp.bfloat16)  7.8 us
    dot_general x1, matrix products, body(): jnp.dot(attended, w_out, preferred_element_type=jnp.float32)  6.5 us
    dot_general x1, local copies, waits for them, and re-layouts, project(): jnp.dot(normed, w_query, preferred_element_type=jnp.float32)  6.39 us
    another operation x1, loops' own time, body(): paired, carry = lax.fori_loop(1, reach + 1, one_step, (paired, carry))  6.03 us
  transfers between devices with their start and end apart: 7, of which 7 were waited for; matrix products, arithmetic and copies ran while one was open for 6% of the time, Pallas kernels for 0%

profile of v1, /device:TPU:0, one launch (start us, length us, event | category | flops | bytes accessed | tf_op | source)
XLA Modules:
  0.0 214.2 jit_solution(3879692780226005350)
XLA Ops:
  6.5 0.0 copy-start
  6.5 3.8 %stack.6 = bf16[4,128,4096]{2,1,0:T(8,128)(2,1)} broadcast(bf16[128,4096]{1,0:T(8,128)(2,1)} %param.13), dimensions={1,2} | broadcast | bytes 5242880 | tf_op jit(solution)/shard_map/stack | solution.py:112
  10.3 5.0 %all-to-all-start = ((bf16[4,128,4096]{2,1,0:T(8,128)(2,1)}), bf16[4,128,4096]{2,1,0:T(8,128)(2,1)}, u32[]{:S(2)}, u32[]{:S(2)}) async-start(bf16[4,128,4096]{2,1,0:T(8,128)(2,1)} %stack.6), calls=%async_computation | async-start | bytes 8388608 | tf_op jit(solution)/shard_map/all_to_all | solution.py:113
  15.3 0.0 reduce-scatter.2.cloned.1.call-start
  15.4 0.5 slice.69
  15.9 0.0 copy-done.5
  15.9 0.2 reduce-window.8
  16.1 0.1 select_reduce_fusion
  16.2 0.5 slice.68
  17.9 6.4 %copy.42 = bf16[512,4096]{1,0:T(8,128)(2,1)} copy(bf16[512,4096]{0,1:T(8,128)(2,1)} %bitcast.154) | data formatting | bytes 8388608 | tf_op jit(solution)/shard_map/dot_general | solution.py:46
  24.3 0.1 broadcast_in_dim.24
  24.4 0.5 multiply_cosine_fusion
  25.0 39.3 %all-to-all-done = bf16[4,128,4096]{2,1,0:T(8,128)(2,1)} async-done(((bf16[4,128,4096]{2,1,0:T(8,128)(2,1)}), bf16[4,128,4096]{2,1,0:T(8,128)(2,1)}, u32[]{:S(2)}, u32[]{:S(2)}) %all-to-all-start) | async-done | bytes 4194336 | tf_op jit(solution)/shard_map/all_to_all | solution.py:113
  64.2 3.1 %multiply_reduce_fusion = f32[4,128]{1,0:T(4,128)S(1)} fusion(bf16[4,128,4096]{2,1,0:T(8,128)(2,1)} %all-to-all-done), kind=kLoop, calls=%fused_computation.49 | loop fusion | flops 6290944 | bytes 4196352 | tf_op jit(solution)/shard_map/reduce_sum | solution.py:43
  67.3 0.0 copy-done.4
  67.3 3.8 %fusion.43 = bf16[512,4096]{1,0:T(8,128)(2,1)S(1)} fusion(bf16[4,128,4096]{2,1,0:T(8,128)(2,1)} %all-to-all-done, f32[4096]{0:T(1024)S(1)} %copy-done.4, f32[512]{0:T(512)S(1)} %get-tuple-element.568), kind=kLoop, calls=%fused_computation.47 | loop fusion | flops 8388608 | bytes 8407040 | tf_op jit(solution)/shard_map/convert_element_type | solution.py:44
  71.1 0.0 copy-done
  71.2 0.0 copy-start.3
  71.2 1.5 convolution_convert_fusion.1
  72.7 1.5 convolution_bitcast_fusion
  74.3 0.6 fusion.51
  74.9 0.8 copy.34
  75.7 4.0 %multiply_convert_fusion = bf16[4,128,4096]{2,1,0:T(8,128)(2,1)S(1)} fusion(bf16[4,128,4096]{2,1,0:T(8,128)(2,1)} %all-to-all-done, f32[4096]{0:T(1024)S(1)} %copy-done.4, f32[4,128]{1,0:T(4,128)S(1)} %get-tuple-element.567), kind=kLoop, calls=%fused_computation.48 | loop fusion | flops 8388608 | bytes 8407040 | tf_op jit(solution)/shard_map/convert_element_type | solution.py:44
  79.7 2.4 %fusion.55 = f32[512,4,128]{0,2,1:T(8,128)S(1)} fusion(bf16[512,4096,1]{1,0,2:T(8,128)(2,1)S(1)} %bitcast.153, bf16[4,128,4096]{2,1,0:T(8,128)(2,1)S(1)} %bitcast.155), kind=kOutput, calls=%fused_computation.80 | convolution fusion | flops 2147483648 | bytes 9437184 | tf_op jit(solution)/shard_map/dot_general | solution.py:46
  82.1 0.2 fusion.44
  82.3 0.3 copy.35
  82.6 4.0 %conditional.2 = ((f32[512,1,4]{0,2,1:T(4,128)S(1)}, f32[512,1,4]{0,2,1:T(4,128)S(1)}, f32[512,1,4,128]{3,0,2,1:T(8,128)S(1)})) conditional(s32[]{:T(128)} %convert_element_type.103, (f32[512,1,4]{0,2,1:T(4,128)S(1)}, f32[512,1,4]{0,2,1:T(4,128)S(1)}, f32[512,1,4,128]{3,0,2,1:T(8,128)S(1)}) %tuple.55, (s32[512]{0:T(512)S(1)}, s32[512]{0:T(512)S(1)}, ...), branch_computations={%region_3.4_spmd, %region_4.7_spmd} | conditional | flops 549722112 | bytes 16650272 | solution.py:94
  82.8 0.3 compare_and_fusion
  83.1 0.9 fusion.2
  84.0 0.9 fusion.1
  84.9 1.6 fusion.10
  86.6 56.9 %while.45 = (s32[]{:T(128)}, bf16[2,512,128]{2,1,0:T(8,128)(2,1)}, f32[512,1,4]{0,2,1:T(4,128)S(1)}, f32[512,1,4]{0,2,1:T(4,128)S(1)}, f32[512,1,4,128]{3,0,2,1:...) while((s32[]{:T(128)}, bf16[2,512,128]{2,1,0:T(8,128)(2,1)}, ...), condition=%wide.region_12.13_spmd, body=%wide.region_7.12_spmd.sunk | while | flops 549722624 | bytes 18231664 | solution.py:140
  86.6 4.2 %collective-permute-start = (bf16[2,512,128]{2,1,0:T(8,128)(2,1)}, bf16[2,512,128]{2,1,0:T(8,128)(2,1)S(1)}, u32[]{:S(2)}, u32[]{:S(2)}) collective-permute-start(bf16[2,512,128]{2,1,0:T(8,128)(2,1)} %get-tuple-element.655), channel_id=1, source_target_pairs={{0,4},{4,8},{8,12},{12,16},{16,20},{20,24},{24,28},{1,5},{5,9},{9,... | collective-permute-start | bytes 786440 | tf_op jit(solution)/shard_map/while/body/eval_jaxpr/ppermute | solution.py:16
  90.8 0.5 slice.104
  91.3 0.6 slice.105
  93.0 3.3 %collective-permute-done = bf16[2,512,128]{2,1,0:T(8,128)(2,1)S(1)} collective-permute-done((bf16[2,512,128]{2,1,0:T(8,128)(2,1)}, bf16[2,512,128]{2,1,0:T(8,128)(2,1)S(1)}, u32[]{:S(2)}, u32[]{:S(2)}) %collective-permute-start) | collective-permute-done | bytes 262176 | tf_op jit(solution)/shard_map/while/body/eval_jaxpr/ppermute | solution.py:16
  96.3 0.7 copy.66
  97.0 8.0 %collective-permute-start = (bf16[2,512,128]{2,1,0:T(8,128)(2,1)}, bf16[2,512,128]{2,1,0:T(8,128)(2,1)S(1)}, u32[]{:S(2)}, u32[]{:S(2)}) collective-permute-start(bf16[2,512,128]{2,1,0:T(8,128)(2,1)} %get-tuple-element.655), channel_id=1, source_target_pairs={{0,4},{4,8},{8,12},{12,16},{16,20},{20,24},{24,28},{1,5},{5,9},{9,... | collective-permute-start | bytes 786440 | tf_op jit(solution)/shard_map/while/body/eval_jaxpr/ppermute | solution.py:16
  105.0 0.5 slice.104
  105.5 0.6 slice.105
  107.3 2.4 %collective-permute-done = bf16[2,512,128]{2,1,0:T(8,128)(2,1)S(1)} collective-permute-done((bf16[2,512,128]{2,1,0:T(8,128)(2,1)}, bf16[2,512,128]{2,1,0:T(8,128)(2,1)S(1)}, u32[]{:S(2)}, u32[]{:S(2)}) %collective-permute-start) | collective-permute-done | bytes 262176 | tf_op jit(solution)/shard_map/while/body/eval_jaxpr/ppermute | solution.py:16
  109.7 0.7 copy.66
  110.4 4.4 %collective-permute-start = (bf16[2,512,128]{2,1,0:T(8,128)(2,1)}, bf16[2,512,128]{2,1,0:T(8,128)(2,1)S(1)}, u32[]{:S(2)}, u32[]{:S(2)}) collective-permute-start(bf16[2,512,128]{2,1,0:T(8,128)(2,1)} %get-tuple-element.655), channel_id=1, source_target_pairs={{0,4},{4,8},{8,12},{12,16},{16,20},{20,24},{24,28},{1,5},{5,9},{9,... | collective-permute-start | bytes 786440 | tf_op jit(solution)/shard_map/while/body/eval_jaxpr/ppermute | solution.py:16
  114.7 0.5 slice.104
  115.3 0.6 slice.105
  117.0 1.9 collective-permute-done
  118.9 0.7 copy.66
  119.6 8.8 %collective-permute-start = (bf16[2,512,128]{2,1,0:T(8,128)(2,1)}, bf16[2,512,128]{2,1,0:T(8,128)(2,1)S(1)}, u32[]{:S(2)}, u32[]{:S(2)}) collective-permute-start(bf16[2,512,128]{2,1,0:T(8,128)(2,1)} %get-tuple-element.655), channel_id=1, source_target_pairs={{0,4},{4,8},{8,12},{12,16},{16,20},{20,24},{24,28},{1,5},{5,9},{9,... | collective-permute-start | bytes 786440 | tf_op jit(solution)/shard_map/while/body/eval_jaxpr/ppermute | solution.py:16
  128.5 0.5 slice.104
  129.0 0.6 slice.105
  130.8 1.9 collective-permute-done
  132.7 0.7 copy.66
  133.4 5.2 %collective-permute-start = (bf16[2,512,128]{2,1,0:T(8,128)(2,1)}, bf16[2,512,128]{2,1,0:T(8,128)(2,1)S(1)}, u32[]{:S(2)}, u32[]{:S(2)}) collective-permute-start(bf16[2,512,128]{2,1,0:T(8,128)(2,1)} %get-tuple-element.655), channel_id=1, source_target_pairs={{0,4},{4,8},{8,12},{12,16},{16,20},{20,24},{24,28},{1,5},{5,9},{9,... | collective-permute-start | bytes 786440 | tf_op jit(solution)/shard_map/while/body/eval_jaxpr/ppermute | solution.py:16
  138.6 0.5 slice.104
  139.1 0.6 slice.105
  140.8 1.9 collective-permute-done
  142.7 0.7 copy.66
  143.4 0.3 copy.36
  143.8 0.1 divide_convert_fusion
  143.9 6.5 %convolution_convert_fusion = bf16[512,4096]{1,0:T(8,128)(2,1)} fusion(bf16[512,512]{0,1:T(8,128)(2,1)S(1)} %bitcast.158, bf16[512,4096]{1,0:T(8,128)(2,1)} %param.18), kind=kOutput, calls=%fused_computation.50 | convolution fusion | flops 2149580800 | bytes 8912896 | tf_op jit(solution)/shard_map/dot_general | solution.py:144
  150.4 0.0 reduce-scatter.2.cloned.1.call-update
  150.4 54.5 %reduce-scatter.2.cloned.1.call-done = bf16[128,4096]{1,0:T(8,128)(2,1)} async-done(((bf16[512,4096]{1,0:T(8,128)(2,1)}), bf16[128,4096]{1,0:T(8,128)(2,1)}) %reduce-scatter.2.cloned.1.call-update) | async-done | bytes 1048592 | tf_op jit(solution)/shard_map/reduce_scatter | solution.py:143
  204.9 0.0 copy-done.1
  204.9 2.4 %add_convert_fusion = bf16[128,4096]{1,0:T(8,128)(2,1)} fusion(bf16[128,4096]{1,0:T(8,128)(2,1)} %reduce-scatter.2.cloned.1.call-done, bf16[128,4096]{1,0:T(8,128)(2,1)S(1)} %copy-done.1), kind=kLoop, calls=%fused_computation.51 | loop fusion | flops 2097152 | bytes 3145728 | tf_op jit(solution)/shard_map/convert_element_type | solution.py:149
  (28 shorter events, 0.2 us)
Async XLA Ops:
  6.5 64.6 %copy-start = (bf16[4096,128]{1,0:T(8,128)(2,1)S(1)}, bf16[4096,128]{1,0:T(8,128)(2,1)}, u32[]{:S(2)}) copy-start(bf16[4096,128]{1,0:T(8,128)(2,1)} %param.17) | copy-start | bytes 3145732
  10.3 5.6 %copy-start.5 = (s32[4]{0:T(128)S(1)}, s32[4]{0:T(128)}, u32[]{:S(2)}) copy-start(s32[4]{0:T(128)} %param.19) | copy-start | bytes 52
  10.3 53.9 %all-to-all-start = ((bf16[4,128,4096]{2,1,0:T(8,128)(2,1)}), bf16[4,128,4096]{2,1,0:T(8,128)(2,1)}, u32[]{:S(2)}, u32[]{:S(2)}) async-start(bf16[4,128,4096]{2,1,0:T(8,128)(2,1)} %stack.6), calls=%async_computation | async-start | bytes 8388608 | tf_op jit(solution)/shard_map/all_to_all | solution.py:113
  15.3 189.6 %reduce-scatter.2.cloned.1.call-start = ((), (), s32[]{:S(2)}) async-start(), calls=%async_computation.2 | async-start | bytes 5242880 | tf_op jit(solution)/shard_map/reduce_scatter | solution.py:143
  24.3 43.0 %copy-start.4 = (f32[4096]{0:T(1024)S(1)}, f32[4096]{0:T(1024)}, u32[]{:S(2)}) copy-start(f32[4096]{0:T(1024)} %param.14) | copy-start | bytes 49156
  71.2 1.6 copy-start.3
  75.7 4.0 %copy-start.2 = (bf16[512,4096]{1,0:T(8,128)(2,1)S(1)}, bf16[512,4096]{1,0:T(8,128)(2,1)}, u32[]{:S(2)}) copy-start(bf16[512,4096]{1,0:T(8,128)(2,1)} %copy.42) | copy-start | bytes 12582916
  86.6 9.7 %collective-permute-start = (bf16[2,512,128]{2,1,0:T(8,128)(2,1)}, bf16[2,512,128]{2,1,0:T(8,128)(2,1)S(1)}, u32[]{:S(2)}, u32[]{:S(2)}) collective-permute-start(bf16[2,512,128]{2,1,0:T(8,128)(2,1)} %get-tuple-element.655), channel_id=1, source_target_pairs={{0,4},{4,8},{8,12},{12,16},{16,20},{20,24},{24,28},{1,5},{5,9},{9,... | collective-permute-start | bytes 786440 | tf_op jit(solution)/shard_map/while/body/eval_jaxpr/ppermute | solution.py:16
  97.0 12.7 %collective-permute-start = (bf16[2,512,128]{2,1,0:T(8,128)(2,1)}, bf16[2,512,128]{2,1,0:T(8,128)(2,1)S(1)}, u32[]{:S(2)}, u32[]{:S(2)}) collective-permute-start(bf16[2,512,128]{2,1,0:T(8,128)(2,1)} %get-tuple-element.655), channel_id=1, source_target_pairs={{0,4},{4,8},{8,12},{12,16},{16,20},{20,24},{24,28},{1,5},{5,9},{9,... | collective-permute-start | bytes 786440 | tf_op jit(solution)/shard_map/while/body/eval_jaxpr/ppermute | solution.py:16
  110.4 8.5 %collective-permute-start = (bf16[2,512,128]{2,1,0:T(8,128)(2,1)}, bf16[2,512,128]{2,1,0:T(8,128)(2,1)S(1)}, u32[]{:S(2)}, u32[]{:S(2)}) collective-permute-start(bf16[2,512,128]{2,1,0:T(8,128)(2,1)} %get-tuple-element.655), channel_id=1, source_target_pairs={{0,4},{4,8},{8,12},{12,16},{16,20},{20,24},{24,28},{1,5},{5,9},{9,... | collective-permute-start | bytes 786440 | tf_op jit(solution)/shard_map/while/body/eval_jaxpr/ppermute | solution.py:16
  119.6 13.0 %collective-permute-start = (bf16[2,512,128]{2,1,0:T(8,128)(2,1)}, bf16[2,512,128]{2,1,0:T(8,128)(2,1)S(1)}, u32[]{:S(2)}, u32[]{:S(2)}) collective-permute-start(bf16[2,512,128]{2,1,0:T(8,128)(2,1)} %get-tuple-element.655), channel_id=1, source_target_pairs={{0,4},{4,8},{8,12},{12,16},{16,20},{20,24},{24,28},{1,5},{5,9},{9,... | collective-permute-start | bytes 786440 | tf_op jit(solution)/shard_map/while/body/eval_jaxpr/ppermute | solution.py:16
  133.4 9.4 %collective-permute-start = (bf16[2,512,128]{2,1,0:T(8,128)(2,1)}, bf16[2,512,128]{2,1,0:T(8,128)(2,1)S(1)}, u32[]{:S(2)}, u32[]{:S(2)}) collective-permute-start(bf16[2,512,128]{2,1,0:T(8,128)(2,1)} %get-tuple-element.655), channel_id=1, source_target_pairs={{0,4},{4,8},{8,12},{12,16},{16,20},{20,24},{24,28},{1,5},{5,9},{9,... | collective-permute-start | bytes 786440 | tf_op jit(solution)/shard_map/while/body/eval_jaxpr/ppermute | solution.py:16
  150.4 54.5 %copy-start.1 = (bf16[128,4096]{1,0:T(8,128)(2,1)S(1)}, bf16[128,4096]{1,0:T(8,128)(2,1)}, u32[]{:S(2)}) copy-start(bf16[128,4096]{1,0:T(8,128)(2,1)} %param.13) | copy-start | bytes 3145732
Sparse Core Ops, SparseCore 0:
  150.6 54.3 reduce-scatter.1
